TPU v7x, 256 devices: a whole 4x4x8 slice. The times are simulated.
256 devices in a mesh: energy: 128 (over z, y, x), mom: 2 (over core).
Axes of the slice: x: 4, y: 4, z: 8, core: 2. Of those that a mesh axis runs over, the one named last changes fastest.
Arguments:
- lesser: bfloat16 [2, 2, 512, 65536], P('mom', None, 'energy'), may hold values from -6 to 6
- greater: bfloat16 [2, 2, 512, 65536], P('mom', None, 'energy'), may hold values from -6 to 6
- coulomb: bfloat16 [2, 4, 128, 128], P('mom'), may hold values from -0.375 to 0.375
- tile_block: int32 [4], replicated, may hold values from 0 to 3, each once
- shift_table: int32 [2, 2], replicated, may hold values from 0 to 1, each once within a row
Outputs:
- polarization: bfloat16 [2, 2, 512, 65536], P('mom', None, 'energy')
- screened: float32 [2, 2, 128, 65536], P('mom', None, 'energy')
Inputs may be any that keep to these rules, and one draw needn't show every extreme that they name: `tile_block`: each of the 4 tiles holds a different block of the pattern. `shift_table`: each row names every momentum once.
All inputs are finite; a program needn't handle non-finite values.
Results may differ from a plain program's by a relative error of at most 0.0013.
Values may be sent and summed in bfloat16 or wider, within the bound.
A program may use at most 128 MiB of HBM per device.

v0:
```python
import math
import jax
import jax.numpy as jnp
from jax import lax
from jax.sharding import PartitionSpec as P

E = 512


def rotation(product, period, sign):
    angle = 2.0 * math.pi / period * (product % period).astype(jnp.float32)
    return (jnp.cos(angle), sign * jnp.sin(angle))


def complex_einsum(form, table_re, table_im, data_re, data_im, data_axis):
    upper = jnp.concatenate((table_re, -table_im), axis=1)
    lower = jnp.concatenate((table_im, table_re), axis=1)
    table = jnp.concatenate((upper, lower), axis=0)
    data = jnp.concatenate((data_re, data_im), axis=data_axis)
    result = jnp.einsum(
        form, table, data, precision=lax.Precision.HIGH, preferred_element_type=jnp.float32
    )
    half = table_re.shape[0]
    return (result[:half], result[half:])


def transform(data_re, data_im, length, sign):
    radix = 32
    rows, width = data_re.shape
    outer = length // radix
    inner = rows // radix
    shaped_re = data_re.reshape(inner, radix, width)
    shaped_im = data_im.reshape(inner, radix, width)
    freq = jnp.arange(outer, dtype=jnp.int32)
    first_re, first_im = rotation(
        freq[:, None] * jnp.arange(inner, dtype=jnp.int32)[None, :], outer, sign
    )
    mid_re, mid_im = complex_einsum("kn,nmc->kmc", first_re, first_im, shaped_re, shaped_im, 0)
    twist_re, twist_im = rotation(
        freq[:, None] * jnp.arange(radix, dtype=jnp.int32)[None, :], length, sign
    )
    turned_re = mid_re * twist_re[:, :, None] - mid_im * twist_im[:, :, None]
    turned_im = mid_re * twist_im[:, :, None] + mid_im * twist_re[:, :, None]
    digits = jnp.arange(radix, dtype=jnp.int32)
    last_re, last_im = rotation(digits[:, None] * digits[None, :], radix, sign)
    out_re, out_im = complex_einsum("jm,kmc->jkc", last_re, last_im, turned_re, turned_im, 1)
    return (out_re.reshape(length, width), out_im.reshape(length, width))


def spectrum(pair, energies):
    return transform(pair[0].astype(jnp.float32), pair[1].astype(jnp.float32), 2 * energies, -1.0)


def correlate(left, right, rows, energies):
    count = left.shape[0]
    spec_left = [spectrum(left[k], energies) for k in range(count)]
    spec_right = [spectrum(right[k], energies) for k in range(count)]
    right_re = jnp.stack([item[0] for item in spec_right])
    right_im = jnp.stack([item[1] for item in spec_right])
    scale = 1.0 / (math.sqrt(count * energies) * 2 * energies)
    total_re = jnp.zeros_like(spec_left[0][0])
    total_im = jnp.zeros_like(spec_left[0][0])
    for k in range(count):
        other_re = lax.dynamic_index_in_dim(right_re, rows[0, k], 0, keepdims=False)
        other_im = lax.dynamic_index_in_dim(right_im, rows[0, k], 0, keepdims=False)
        total_re = total_re + spec_left[k][0] * other_re + spec_left[k][1] * other_im
        total_im = total_im + spec_left[k][1] * other_re - spec_left[k][0] * other_im
    back_re, back_im = transform(total_re, total_im, 2 * energies, 1.0)
    results = [jnp.stack([-back_im[:energies], back_re[:energies]]) * scale]
    return jnp.stack(results)


def polar_all(left, right, rows, energies):
    columns = left.shape[3]
    width = math.gcd(columns, 128)
    count_q = rows.shape[0]

    def step(index, result):
        start = index * width
        part_left = lax.dynamic_slice_in_dim(left, start, width, 3)
        part_right = lax.dynamic_slice_in_dim(right, start, width, 3)
        block = correlate(part_left, part_right, rows, energies).astype(jnp.bfloat16)
        return lax.dynamic_update_slice_in_dim(result, block, start, 3)

    empty = jnp.zeros((count_q, 2, energies, columns), jnp.bfloat16)
    return lax.fori_loop(0, columns // width, step, empty)


def screen(near, coulomb, tile_block):
    tiles_n = coulomb.shape[1]
    block = coulomb.shape[2]
    band = (tiles_n + 2) // 3
    levels = near.shape[2]
    tiles = near[0].reshape(2, levels, tiles_n, block, block)
    labels = jnp.arange(tiles_n, dtype=jnp.int32)
    onehot = tile_block[:, None] == labels[None, :]
    inverse = jnp.sum(jnp.where(onehot, labels[:, None], 0), axis=0)
    ordered = jnp.take(tiles, inverse, axis=2)
    results = []
    for r in range(band):
        for c in range(max(0, r - 1), min(band, r + 2)):
            acc = jnp.zeros((2, levels, block, block), jnp.float32)
            for l in range(max(0, r - 1), min(band, r + 2)):
                acc = acc + jnp.einsum(
                    "ij,sejk->seik",
                    coulomb[0, 2 * r + l],
                    ordered[:, :, 2 * l + c],
                    preferred_element_type=jnp.float32,
                )
            results.append(acc)
    return jnp.stack(results, axis=2).reshape(1, 2, levels, tiles_n * block * block)


def shards(lesser, greater, coulomb, tile_block, shift_table):
    left, right = (
        lax.all_to_all(lesser, "energy", split_axis=3, concat_axis=2, tiled=True),
        lax.all_to_all(greater, "energy", split_axis=3, concat_axis=2, tiled=True),
    )
    left_all, right_all = (
        lax.all_gather(left, "mom", axis=0, tiled=True),
        lax.all_gather(right, "mom", axis=0, tiled=True),
    )
    rows = lax.dynamic_slice_in_dim(shift_table, lax.axis_index("mom"), 1, 0)
    polar_cols = polar_all(left_all, right_all, rows, E)
    polarization = lax.all_to_all(polar_cols, "energy", split_axis=2, concat_axis=3, tiled=True)
    near = lax.all_to_all(
        polar_cols[:, :, : E // 4], "energy", split_axis=2, concat_axis=3, tiled=True
    )
    return (polarization, screen(near, coulomb, tile_block))


def solution(mesh):
    return jax.shard_map(
        shards,
        mesh=mesh,
        in_specs=(
            P("mom", None, "energy", None),
            P("mom", None, "energy", None),
            P("mom", None, None, None),
            P(),
            P(),
        ),
        out_specs=(P("mom", None, "energy", None), P("mom", None, "energy", None)),
        check_vma=False,
    )
```

profile of v0, /device:TPU:32, one launch (start us, length us, event | category | flops | bytes accessed | tf_op | source)
XLA Modules:
  0.0 771.1 jit_solution(1303767852040457556)
XLA Ops:
  7.2 58.7 %copy.125 = bf16[1,2,4,65536]{2,1,0,3:T(2,128)(2,1)} copy(bf16[1,2,4,65536]{3,2,1,0:T(4,128)(2,1)} %param.7) | data formatting | bytes 2097152 | tf_op args[0]
  65.9 61.1 %reshape.429 = bf16[128,2,2048]{2,1,0:T(2,128)(2,1)S(1)} reshape(bf16[65536,1,2,4]{3,2,1,0:T(2,128)(2,1)} %bitcast.190) | data formatting | bytes 2097152
  127.1 46.2 %all_to_all.63 = bf16[128,2,2048]{2,1,0:T(2,128)(2,1)S(1)} all-to-all(bf16[128,2,2048]{2,1,0:T(2,128)(2,1)S(1)} %reshape.429), channel_id=1, replica_groups=mesh['energy'=128,'mom'=2] {'energy'}, dimensions={0} | all-to-all | bytes 2097152 | tf_op jit(solution)/shard_map/all_to_all | solution.py:116
  173.2 73.1 %reshape.430 = bf16[65536,1,2,4]{3,2,1,0:T(2,128)(2,1)} reshape(bf16[128,2,2048]{2,1,0:T(2,128)(2,1)S(1)} %all_to_all.63) | data formatting | bytes 2097152
  246.3 65.3 %copy.126 = bf16[1,2,128,4,512]{4,3,2,1,0:T(4,128)(2,1)S(1)} copy(bf16[1,2,128,4,512]{3,1,4,2,0:T(2,128)(2,1)} %bitcast.188) | data formatting | bytes 2097152 | tf_op jit(solution)/shard_map/all_to_all | solution.py:116
  312.9 50.9 %copy.127 = bf16[1,2,4,65536]{2,1,0,3:T(2,128)(2,1)} copy(bf16[1,2,4,65536]{3,2,1,0:T(4,128)(2,1)S(1)} %copy-done.2) | data formatting | bytes 2097152 | tf_op args[1]
  363.8 61.1 %reshape.431 = bf16[128,2,2048]{2,1,0:T(2,128)(2,1)S(1)} reshape(bf16[65536,1,2,4]{3,2,1,0:T(2,128)(2,1)} %bitcast.191) | data formatting | bytes 2097152
  424.9 36.4 %all_to_all.64 = bf16[128,2,2048]{2,1,0:T(2,128)(2,1)S(1)} all-to-all(bf16[128,2,2048]{2,1,0:T(2,128)(2,1)S(1)} %reshape.431), channel_id=1, replica_groups=mesh['energy'=128,'mom'=2] {'energy'}, dimensions={0} | all-to-all | bytes 2097152 | tf_op jit(solution)/shard_map/all_to_all | solution.py:117
  461.4 73.1 %reshape.432 = bf16[65536,1,2,4]{3,2,1,0:T(2,128)(2,1)} reshape(bf16[128,2,2048]{2,1,0:T(2,128)(2,1)S(1)} %all_to_all.64) | data formatting | bytes 2097152
  534.5 65.3 %copy.128 = bf16[1,2,128,4,512]{4,3,2,1,0:T(4,128)(2,1)S(1)} copy(bf16[1,2,128,4,512]{3,1,4,2,0:T(2,128)(2,1)} %bitcast.189) | data formatting | bytes 2097152 | tf_op jit(solution)/shard_map/all_to_all | solution.py:117
  605.4 5.2 all-gather.5.cloned.1.call-done
  610.6 1.5 broadcast_in_dim.29.clone
  612.1 82.8 %while.16 = (s32[]{:T(128)}, bf16[1,2,512,512]{3,1,0,2:T(2,128)(2,1)}, bf16[2,2,512,512]{3,2,1,0:T(8,128)(2,1)}, bf16[2,2,512,512]{3,2,1,0:T(8,128)(2,1)}, s32[]...) while((s32[]{:T(128)}, bf16[1,2,512,512]{3,1,0,2:T(2,128)(2,1)}, ...), condition=%wide.region_1.2_spmd, body=%wide.region_0.1_spmd.sunk | while | flops 815953408 | bytes 64403652 | solution.py:86
  612.1 1.2 constant_dynamic-slice_fusion.11
  614.2 1.2 constant_dynamic-slice_fusion.12
  616.8 1.5 fusion.159
  618.7 2.0 multiply_subtract_fusion.8
  621.1 1.2 fusion.170
  623.0 1.2 fusion.168
  627.8 1.3 multiply_add_fusion.7
  634.9 1.2 constant_dynamic-slice_fusion.12
  637.5 1.5 fusion.159
  639.4 2.0 multiply_subtract_fusion.8
  641.7 1.2 fusion.170
  646.2 1.2 fusion.166
  647.3 1.2 fusion.167
  648.5 1.3 multiply_add_fusion.7
  651.1 1.2 fusion.176
  658.2 1.5 fusion.159
  660.1 2.0 multiply_subtract_fusion.8
  662.4 1.2 fusion.170
  666.9 1.2 fusion.166
  668.0 1.2 fusion.167
  669.2 1.3 multiply_add_fusion.7
  676.2 1.2 constant_dynamic-slice_fusion.12
  678.9 1.5 fusion.159
  680.7 2.0 multiply_subtract_fusion.8
  683.1 1.2 fusion.170
  687.5 1.2 fusion.166
  688.7 1.2 fusion.167
  689.9 1.3 multiply_add_fusion.7
  692.5 1.2 fusion.176
  694.9 1.8 slice.403
  696.7 13.7 %all-to-all-start.3 = ((bf16[1,2,128,512]{3,1,0,2:T(2,128)(2,1)}), bf16[1,2,128,512]{3,1,0,2:T(2,128)(2,1)S(1)}, u32[]{:S(2)}, u32[]{:S(2)}) async-start(bf16[1,2,128,512]{3,1,0,2:T(2,128)(2,1)} %slice.403), calls=%async_computation.3 | async-start | bytes 524288 | tf_op jit(solution)/shard_map/all_to_all | solution.py:126
  710.6 15.1 %all-to-all-done.3 = bf16[1,2,128,512]{3,1,0,2:T(2,128)(2,1)S(1)} async-done(((bf16[1,2,128,512]{3,1,0,2:T(2,128)(2,1)}), bf16[1,2,128,512]{3,1,0,2:T(2,128)(2,1)S(1)}, u32[]{:S(2)}, u32[]{:S(2)}) %all-to-all-start.3) | async-done | bytes 262176 | tf_op jit(solution)/shard_map/all_to_all | solution.py:126
  725.7 6.5 all-to-all-start.2
  735.8 26.6 %all-to-all-done.2 = bf16[1,2,512,512]{3,1,0,2:T(2,128)(2,1)S(1)} async-done(((bf16[1,2,512,512]{3,1,0,2:T(2,128)(2,1)}), bf16[1,2,512,512]{3,1,0,2:T(2,128)(2,1)S(1)}, u32[]{:S(2)}, u32[]{:S(2)}) %all-to-all-start.2) | async-done | bytes 1048608 | tf_op jit(solution)/shard_map/all_to_all | solution.py:125
  762.7 1.6 all_to_all.57
  (218 shorter events, 49.5 us)
Async XLA Ops:
  7.2 593.8 %copy-start = (s32[2,2]{1,0:T(2,128)S(1)}, s32[2,2]{1,0:T(2,128)}, u32[]{:S(2)}) copy-start(s32[2,2]{1,0:T(2,128)} %param.11) | copy-start | bytes 52
  7.2 598.2 %all-gather.3.cloned.1.call-start = ((), (), s32[]{:S(2)}) async-start(), calls=%async_computation.4 | async-start | bytes 3145728 | tf_op jit(solution)/shard_map/all_gather | solution.py:120
  173.2 139.6 %copy-start.2 = (bf16[1,2,4,65536]{3,2,1,0:T(4,128)(2,1)S(1)}, bf16[1,2,4,65536]{3,2,1,0:T(4,128)(2,1)}, u32[]{:S(2)}) copy-start(bf16[1,2,4,65536]{3,2,1,0:T(4,128)(2,1)} %param.8) | copy-start | bytes 3145732
  312.8 297.8 %all-gather.5.cloned.1.call-start = ((), (), s32[]{:S(2)}) async-start(), calls=%async_computation.5 | async-start | bytes 3145728 | tf_op jit(solution)/shard_map/all_gather | solution.py:121
  612.1 98.3 %copy-start.4 = (s32[4]{0:T(128)S(1)}, s32[4]{0:T(128)}, u32[]{:S(2)}) copy-start(s32[4]{0:T(128)} %param.10) | copy-start | bytes 52
  612.1 121.3 %copy-start.3 = (bf16[1,4,128,128]{3,2,1,0:T(8,128)(2,1)S(1)}, bf16[1,4,128,128]{3,2,1,0:T(8,128)(2,1)}, u32[]{:S(2)}) copy-start(bf16[1,4,128,128]{3,2,1,0:T(8,128)(2,1)} %param.9) | copy-start | bytes 393220
  694.9 69.4 %copy-start.1 = (s32[2,2]{1,0:T(2,128)S(1)}, s32[2,2]{1,0:T(2,128)}, u32[]{:S(2)}) copy-start(s32[2,2]{1,0:T(2,128)} %param.11) | copy-start | bytes 52
  696.7 28.9 %all-to-all-start.3 = ((bf16[1,2,128,512]{3,1,0,2:T(2,128)(2,1)}), bf16[1,2,128,512]{3,1,0,2:T(2,128)(2,1)S(1)}, u32[]{:S(2)}, u32[]{:S(2)}) async-start(bf16[1,2,128,512]{3,1,0,2:T(2,128)(2,1)} %slice.403), calls=%async_computation.3 | async-start | bytes 524288 | tf_op jit(solution)/shard_map/all_to_all | solution.py:126
  725.7 36.7 %all-to-all-start.2 = ((bf16[1,2,512,512]{3,1,0,2:T(2,128)(2,1)}), bf16[1,2,512,512]{3,1,0,2:T(2,128)(2,1)S(1)}, u32[]{:S(2)}, u32[]{:S(2)}) async-start(bf16[1,2,512,512]{3,1,0,2:T(2,128)(2,1)} %get-tuple-element.179), calls=%async_computation.2 | async-start | bytes 2097152 | tf_op jit(solution)/shard_map/all_to_all | solution.py:125
Sparse Core Ops, SparseCore 0:
  312.9 9.4 all-gather.2
  601.1 9.4 all-gather.4
where the time goes:
time: 779 us; the launch traced here: 771 us
  local copies, waits for them, and re-layouts  541 us (69%)
  blocking collectives  82.6 us (11%)
  waiting for transfers between devices  47 us (6%)
  matrix products  39.7 us (5%)
  other arithmetic  21.5 us (3%)
  starting transfers between devices  20.3 us (3%)
  between operations  18 us (2%)
    unnamed x16, local copies, waits for them, and re-layouts  378 us
    all_to_all x2, local copies, waits for them, and re-layouts, shards(): lax.all_to_all(greater, 'energy', split_axis=3, concat_axis=2, tiled=True)  66.5 us
    all_to_all x2, local copies, waits for them, and re-layouts, shards(): lax.all_to_all(lesser, 'energy', split_axis=3, concat_axis=2, tiled=True)  66.4 us
    all_to_all x1, blocking collectives, shards(): lax.all_to_all(lesser, 'energy', split_axis=3, concat_axis=2, tiled=True)  46.2 us
    dot_general x40, matrix products, complex_einsum(): jnp.einsum(form, table, data, precision=lax.Precision.HIGH, preferred_ele...  38.4 us
    all_to_all x1, blocking collectives, shards(): lax.all_to_all(greater, 'energy', split_axis=3, concat_axis=2, tiled=True)  36.4 us
    all_to_all x1, waiting for transfers between devices, shards(): lax.all_to_all(polar_cols, 'energy', split_axis=2, concat_axis=3, tiled=T...  26.6 us
  transfers between devices with their start and end apart: 4, of which 3 were waited for; matrix products, arithmetic and copies ran while one was open for 33% of the time, Pallas kernels for 0%

commit v1 on v0

--- a/solution.py
+++ b/solution.py
@@ -5,6 +5,13 @@
 from jax.sharding import PartitionSpec as P
 
 E = 512
+
+
+def trade_parts(value, axis, split, join):
+    devices = lax.axis_size(axis)
+    tiles = jnp.stack(jnp.split(value, devices, axis=split), axis=0)
+    tiles = lax.all_to_all(tiles, axis, split_axis=0, concat_axis=0)
+    return jnp.concatenate(tiles, axis=join)
 
 
 def rotation(product, period, sign):
@@ -113,7 +120,7 @@
 
 def shards(lesser, greater, coulomb, tile_block, shift_table):
     left, right = (
-        lax.all_to_all(lesser, "energy", split_axis=3, concat_axis=2, tiled=True),
+        trade_parts(lesser, "energy", 3, 2),
         lax.all_to_all(greater, "energy", split_axis=3, concat_axis=2, tiled=True),
     )
     left_all, right_all = (

time: 779 us -> 612 us (0.79)
  local copies, waits for them, and re-layouts: 541 us -> 374 us
    unnamed x16 -> x140, local copies, waits for them, and re-layouts: 378 us -> 275 us
    all_to_all x2 -> x0, local copies, waits for them, and re-layouts: 66.4 us -> none  [shards(): lax.all_to_all(lesser, 'energy', split_axis=3, concat_axis=2, tiled=True)]
  transfers between devices with their start and end apart: 4 -> 4, of which waited for: 3 -> 3; matrix products, arithmetic and copies ran while one was open for 33% -> 42% of each run, Pallas kernels for 0% -> 0%
where the time goes in v1:
time: 612 us; the launch traced here: 604 us
  local copies, waits for them, and re-layouts  374 us (61%)
  blocking collectives  82.6 us (13%)
  waiting for transfers between devices  47 us (8%)
  matrix products  39.8 us (7%)
  other arithmetic  21.5 us (4%)
  starting transfers between devices  20.3 us (3%)
  between operations  18.1 us (3%)
    unnamed x140, local copies, waits for them, and re-layouts  275 us
    all_to_all x2, local copies, waits for them, and re-layouts, shards(): lax.all_to_all(greater, 'energy', split_axis=3, concat_axis=2, tiled=True)  66.5 us
    all_to_all x1, blocking collectives, trade_parts(): tiles = lax.all_to_all(tiles, axis, split_axis=0, concat_axis=0)  46.1 us
    dot_general x40, matrix products, complex_einsum(): jnp.einsum(form, table, data, precision=lax.Precision.HIGH, preferred_ele...  38.5 us
    all_to_all x1, blocking collectives, shards(): lax.all_to_all(greater, 'energy', split_axis=3, concat_axis=2, tiled=True)  36.4 us
    all_to_all x1, waiting for transfers between devices, shards(): lax.all_to_all(polar_cols, 'energy', split_axis=2, concat_axis=3, tiled=T...  26.6 us
    all_to_all x1, waiting for transfers between devices, shards(): lax.all_to_all(polar_cols[:, :, :E // 4], 'energy', split_axis=2, concat_...  15.1 us
    all_to_all x1, starting transfers between devices, shards(): lax.all_to_all(polar_cols[:, :, :E // 4], 'energy', split_axis=2, concat_...  13.7 us
  transfers between devices with their start and end apart: 4, of which 3 were waited for; matrix products, arithmetic and copies ran while one was open for 42% of the time, Pallas kernels for 0%

profile of v1, /device:TPU:32, one launch (start us, length us, event | category | flops | bytes accessed | tf_op | source)
XLA Modules:
  0.0 604.3 jit_solution(5182563067995911619)
XLA Ops:
  98.0 46.1 %all_to_all.50 = bf16[128,1,2,4,512]{4,3,2,1,0:T(4,128)(2,1)S(1)} all-to-all(bf16[128,1,2,4,512]{4,3,2,1,0:T(4,128)(2,1)S(1)} %constant_dynamic-update-slice_fusion), channel_id=1, replica_groups=mesh['energy'=128,'mom'=2] {'energy'}, dimensions={0} | all-to-all | bytes 2097152 | tf_op jit(solution)/shard_map/all_to_all | solution.py:13
  146.1 50.8 %copy.125 = bf16[1,2,4,65536]{2,1,0,3:T(2,128)(2,1)} copy(bf16[1,2,4,65536]{3,2,1,0:T(4,128)(2,1)S(1)} %copy-done.2) | data formatting | bytes 2097152 | tf_op args[1]
  196.9 61.1 %reshape.437 = bf16[128,2,2048]{2,1,0:T(2,128)(2,1)S(1)} reshape(bf16[65536,1,2,4]{3,2,1,0:T(2,128)(2,1)} %bitcast.441) | data formatting | bytes 2097152
  258.0 36.4 %all_to_all.51 = bf16[128,2,2048]{2,1,0:T(2,128)(2,1)S(1)} all-to-all(bf16[128,2,2048]{2,1,0:T(2,128)(2,1)S(1)} %reshape.437), channel_id=1, replica_groups=mesh['energy'=128,'mom'=2] {'energy'}, dimensions={0} | all-to-all | bytes 2097152 | tf_op jit(solution)/shard_map/all_to_all | solution.py:124
  294.5 73.1 %reshape.438 = bf16[65536,1,2,4]{3,2,1,0:T(2,128)(2,1)} reshape(bf16[128,2,2048]{2,1,0:T(2,128)(2,1)S(1)} %all_to_all.51) | data formatting | bytes 2097152
  367.6 65.3 %copy.126 = bf16[1,2,128,4,512]{4,3,2,1,0:T(4,128)(2,1)S(1)} copy(bf16[1,2,128,4,512]{3,1,4,2,0:T(2,128)(2,1)} %bitcast.440) | data formatting | bytes 2097152 | tf_op jit(solution)/shard_map/all_to_all | solution.py:124
  438.5 5.2 all-gather.5.cloned.1.call-done
  443.7 1.5 broadcast_in_dim.29.clone
  445.2 82.8 %while.16 = (s32[]{:T(128)}, bf16[1,2,512,512]{3,1,0,2:T(2,128)(2,1)}, bf16[2,2,512,512]{3,2,1,0:T(8,128)(2,1)}, bf16[2,2,512,512]{3,2,1,0:T(8,128)(2,1)}, s32[]...) while((s32[]{:T(128)}, bf16[1,2,512,512]{3,1,0,2:T(2,128)(2,1)}, ...), condition=%wide.region_1.2_spmd, body=%wide.region_0.1_spmd.sunk | while | flops 815953408 | bytes 64403652 | solution.py:93
  445.2 1.2 constant_dynamic-slice_fusion.11
  447.3 1.2 constant_dynamic-slice_fusion.12
  449.9 1.5 fusion.159
  451.8 2.0 multiply_subtract_fusion.8
  454.2 1.2 fusion.170
  456.1 1.2 fusion.168
  458.6 1.2 fusion.166
  459.8 1.2 fusion.167
  460.9 1.3 multiply_add_fusion.7
  463.5 1.2 fusion.176
  468.0 1.2 constant_dynamic-slice_fusion.12
  470.6 1.5 fusion.159
  472.5 2.0 multiply_subtract_fusion.8
  474.9 1.2 fusion.170
  476.8 1.2 fusion.168
  479.3 1.2 fusion.166
  480.5 1.2 fusion.167
  481.6 1.3 multiply_add_fusion.7
  484.2 1.2 fusion.176
  491.3 1.5 fusion.159
  493.2 2.0 multiply_subtract_fusion.8
  495.6 1.2 fusion.170
  497.5 1.2 fusion.168
  500.0 1.2 fusion.166
  501.2 1.2 fusion.167
  502.3 1.3 multiply_add_fusion.7
  512.0 1.5 fusion.159
  513.9 2.0 multiply_subtract_fusion.8
  516.3 1.2 fusion.170
  518.2 1.2 fusion.168
  520.7 1.2 fusion.166
  521.9 1.2 fusion.167
  523.0 1.3 multiply_add_fusion.7
  528.1 1.8 slice.403
  529.9 13.7 %all-to-all-start.3 = ((bf16[1,2,128,512]{3,1,0,2:T(2,128)(2,1)}), bf16[1,2,128,512]{3,1,0,2:T(2,128)(2,1)S(1)}, u32[]{:S(2)}, u32[]{:S(2)}) async-start(bf16[1,2,128,512]{3,1,0,2:T(2,128)(2,1)} %slice.403), calls=%async_computation.3 | async-start | bytes 524288 | tf_op jit(solution)/shard_map/all_to_all | solution.py:133
  543.7 15.1 %all-to-all-done.3 = bf16[1,2,128,512]{3,1,0,2:T(2,128)(2,1)S(1)} async-done(((bf16[1,2,128,512]{3,1,0,2:T(2,128)(2,1)}), bf16[1,2,128,512]{3,1,0,2:T(2,128)(2,1)S(1)}, u32[]{:S(2)}, u32[]{:S(2)}) %all-to-all-start.3) | async-done | bytes 262176 | tf_op jit(solution)/shard_map/all_to_all | solution.py:133
  558.8 6.5 %all-to-all-start.2 = ((bf16[1,2,512,512]{3,1,0,2:T(2,128)(2,1)}), bf16[1,2,512,512]{3,1,0,2:T(2,128)(2,1)S(1)}, u32[]{:S(2)}, u32[]{:S(2)}) async-start(bf16[1,2,512,512]{3,1,0,2:T(2,128)(2,1)} %get-tuple-element.179), calls=%async_computation.2 | async-start | bytes 2097152 | tf_op jit(solution)/shard_map/all_to_all | solution.py:132
  568.9 26.6 %all-to-all-done.2 = bf16[1,2,512,512]{3,1,0,2:T(2,128)(2,1)S(1)} async-done(((bf16[1,2,512,512]{3,1,0,2:T(2,128)(2,1)}), bf16[1,2,512,512]{3,1,0,2:T(2,128)(2,1)S(1)}, u32[]{:S(2)}, u32[]{:S(2)}) %all-to-all-start.2) | async-done | bytes 1048608 | tf_op jit(solution)/shard_map/all_to_all | solution.py:132
  595.8 1.6 all_to_all.44
  (343 shorter events, 136.4 us)
Async XLA Ops:
  7.2 426.9 %copy-start = (s32[2,2]{1,0:T(2,128)S(1)}, s32[2,2]{1,0:T(2,128)}, u32[]{:S(2)}) copy-start(s32[2,2]{1,0:T(2,128)} %param.11) | copy-start | bytes 52
  7.2 431.3 %all-gather.3.cloned.1.call-start = ((), (), s32[]{:S(2)}) async-start(), calls=%async_computation.4 | async-start | bytes 3145728 | tf_op jit(solution)/shard_map/all_gather | solution.py:127
  144.5 1.6 copy-start.2
  145.7 298.1 %all-gather.5.cloned.1.call-start = ((), (), s32[]{:S(2)}) async-start(), calls=%async_computation.5 | async-start | bytes 3145728 | tf_op jit(solution)/shard_map/all_gather | solution.py:128
  445.2 98.3 %copy-start.4 = (s32[4]{0:T(128)S(1)}, s32[4]{0:T(128)}, u32[]{:S(2)}) copy-start(s32[4]{0:T(128)} %param.10) | copy-start | bytes 52
  529.9 28.9 %all-to-all-start.3 = ((bf16[1,2,128,512]{3,1,0,2:T(2,128)(2,1)}), bf16[1,2,128,512]{3,1,0,2:T(2,128)(2,1)S(1)}, u32[]{:S(2)}, u32[]{:S(2)}) async-start(bf16[1,2,128,512]{3,1,0,2:T(2,128)(2,1)} %slice.403), calls=%async_computation.3 | async-start | bytes 524288 | tf_op jit(solution)/shard_map/all_to_all | solution.py:133
  543.7 22.8 %copy-start.3 = (bf16[1,4,128,128]{3,2,1,0:T(8,128)(2,1)S(1)}, bf16[1,4,128,128]{3,2,1,0:T(8,128)(2,1)}, u32[]{:S(2)}) copy-start(bf16[1,4,128,128]{3,2,1,0:T(8,128)(2,1)} %param.9) | copy-start | bytes 393220
  558.8 36.7 %all-to-all-start.2 = ((bf16[1,2,512,512]{3,1,0,2:T(2,128)(2,1)}), bf16[1,2,512,512]{3,1,0,2:T(2,128)(2,1)S(1)}, u32[]{:S(2)}, u32[]{:S(2)}) async-start(bf16[1,2,512,512]{3,1,0,2:T(2,128)(2,1)} %get-tuple-element.179), calls=%async_computation.2 | async-start | bytes 2097152 | tf_op jit(solution)/shard_map/all_to_all | solution.py:132
  595.5 1.9 copy-start.1
Sparse Core Ops, SparseCore 0:
  145.8 9.4 all-gather.2
  434.2 9.4 all-gather.4
